TPU v7x, 32 devices: a whole 2x2x4 slice. The times are simulated.
32 devices in a mesh: tok: 4 (over x, core), vocab: 8 (over z, y).
Axes of the slice: x: 2, y: 2, z: 4, core: 2. Of those that a mesh axis runs over, the one named last changes fastest.
Arguments:
- hidden_states: bfloat16 [512, 3584], P('tok'), may hold values from -6 to 6, as said below
- hidden_tangent: bfloat16 [512, 3584], P('tok'), may hold values from -6 to 6
- buckets: int32 [512], P('tok'), may hold values from 0 to 7
- head_weight: bfloat16 [3584, 5120], P(None, 'vocab')
Outputs:
- hidden_cotangent: bfloat16 [3584, 512], P('vocab', 'tok')
- weight_gradient: bfloat16 [3584, 5120], P('tok', 'vocab')
Inputs may be any that keep to these rules, and one draw needn't show every extreme that they name: `hidden_states`: hidden states of order one.
All inputs are finite; a program needn't handle non-finite values.
Results may differ from a plain program's by a relative error of at most 0.0107.
Values may be sent and summed in bfloat16 or wider, within the bound.
A program may use at most 64 MiB of HBM per device.

v0:
```python
import jax
import jax.numpy as jnp
from jax import lax
from jax.sharding import PartitionSpec as P

TOK_DEV = 128
BUCKETS = 8


def local(hidden_states, hidden_tangent, buckets, head_weight):
    logits = jnp.dot(hidden_states, head_weight, preferred_element_type=jnp.float32)
    tangent = jnp.dot(hidden_tangent, head_weight, preferred_element_type=jnp.float32)
    peak = lax.pmax(jnp.max(logits, axis=1), "vocab")
    expo = jnp.exp(logits - peak[:, None])
    total = lax.psum(jnp.sum(expo, axis=1), "vocab")
    probs = expo / total[:, None]
    mean = lax.psum(jnp.sum(probs * tangent, axis=1), "vocab")
    scale = 0.25 * jnp.exp2(buckets.astype(jnp.float32) * (3.0 / (BUCKETS - 1)))
    grads = (scale[:, None] * probs * (tangent - mean[:, None])).astype(jnp.bfloat16)
    width = head_weight.shape[0]
    cotan = lax.psum_scatter(
        lax.dot_general(
            head_weight, grads, (((1,), (1,)), ((), ())), preferred_element_type=jnp.float32
        ),
        "vocab",
        scatter_dimension=0,
        tiled=True,
    )
    hidden_cotangent = cotan.astype(jnp.bfloat16)
    feature_rows = width // lax.axis_size("tok")
    column_start = lax.axis_index("tok") * feature_rows
    pieces = (
        lax.all_gather(hidden_states, "tok", axis=0, tiled=True),
        lax.all_gather(grads, "tok", axis=0, tiled=True),
    )
    columns = lax.dynamic_slice_in_dim(pieces[0], column_start, feature_rows, 1)
    blocks_h = columns.reshape(-1, TOK_DEV, feature_rows)
    blocks_g = pieces[1].reshape(-1, TOK_DEV, pieces[1].shape[1])
    partial_terms = jnp.einsum(
        "kti,ktv->kiv", blocks_h, blocks_g, preferred_element_type=jnp.float32
    ).astype(jnp.bfloat16)
    summed = jnp.sum(partial_terms.astype(jnp.float32), axis=0)
    return (hidden_cotangent, summed.astype(jnp.bfloat16))


def solution(mesh):
    return jax.shard_map(
        local,
        mesh=mesh,
        in_specs=(P("tok", None), P("tok", None), P("tok"), P(None, "vocab")),
        out_specs=(P("vocab", "tok"), P("tok", "vocab")),
        check_vma=False,
    )
```

profile of v0, /device:TPU:0, one launch (start us, length us, event | category | flops | bytes accessed | tf_op | source)
XLA Modules:
  0.0 158.0 jit_solution(476871489584601557)
XLA Ops:
  8.0 0.0 copy-start
  8.0 0.0 reduce-scatter.4.cloned.1.call-start
  8.1 0.7 exponential_multiply_fusion
  8.8 3.6 %fusion.2 = (f32[128]{0:T(128)S(1)}, f32[128,640]{1,0:T(8,128)S(1)}) fusion(bf16[128,3584]{1,0:T(8,128)(2,1)} %param.4, bf16[3584,640]{1,0:T(8,128)(2,1)} %param.7), kind=kOutput, calls=%fused_computation.9 | convolution fusion | flops 587284352 | bytes 5833216 | tf_op jit(solution)/shard_map/dot_general | solution.py:11
  12.3 23.2 %pmax.7 = f32[128]{0:T(128)S(1)} all-reduce(f32[128]{0:T(128)S(1)} %get-tuple-element.8), channel_id=1, replica_groups=mesh['tok'=4,'vocab'=8] {'vocab'}, use_global_device_ids=true, to_apply=%region_1.0 | all-reduce | flops 128 | bytes 1024 | tf_op jit(solution)/shard_map/pmax | solution.py:13
  35.5 0.2 fusion.1
  35.7 17.1 %psum.14 = f32[128]{0:T(128)S(1)} all-reduce(f32[128]{0:T(128)S(1)} %fusion.1), channel_id=1, replica_groups=mesh['tok'=4,'vocab'=8] {'vocab'}, use_global_device_ids=true, to_apply=%region_3.0 | all-reduce | flops 128 | bytes 1024 | tf_op jit(solution)/shard_map/psum | solution.py:15
  52.8 0.0 copy-done
  52.8 3.3 %multiply_reduce_fusion = (f32[128]{0:T(128)S(1)}, f32[128,640]{1,0:T(8,128)S(1)}) fusion(f32[128]{0:T(128)S(1)} %psum.14, f32[128,640]{1,0:T(8,128)S(1)} %get-tuple-element.9, f32[128]{0:T(128)S(1)} %pmax.7, bf16[128,3584]{1,0:T(8,128)(2,1)S(1)} %copy-done, bf16[3584,640]{1,0:T(8,128)(2,1)} %param.7), kind=kOutput, calls=%fused_computation.3 | convolution fusion | flops 587530112 | bytes 6161920 | tf_op jit(solution)/shard_map/dot_general | solution.py:12
  56.1 19.1 %psum.15 = f32[128]{0:T(128)S(1)} all-reduce(f32[128]{0:T(128)S(1)} %get-tuple-element.10), channel_id=1, replica_groups=mesh['tok'=4,'vocab'=8] {'vocab'}, use_global_device_ids=true, to_apply=%region_5.0 | all-reduce | flops 128 | bytes 1024 | tf_op jit(solution)/shard_map/psum | solution.py:17
  75.2 0.2 multiply_convert_fusion
  75.4 3.9 %convolution_bitcast_fusion = f32[3584,128]{0,1:T(8,128)S(1)} fusion(bf16[128,640]{1,0:T(8,128)(2,1)S(1)} %multiply_convert_fusion, bf16[3584,640]{1,0:T(8,128)(2,1)} %param.7), kind=kOutput, calls=%fused_computation | convolution fusion | flops 587202560 | bytes 6586368 | tf_op jit(solution)/shard_map/dot_general | solution.py:22
  79.3 1.7 %copy.12 = f32[3584,128]{1,0:T(8,128)} copy(f32[3584,128]{0,1:T(8,128)S(1)} %convolution_bitcast_fusion) | data formatting | bytes 3670016
  81.0 0.0 reduce-scatter.4.cloned.1.call-update
  81.0 0.0 all-gather.2.cloned.1.call-start
  81.0 0.5 all-gather.2.cloned.1.call-update
  81.6 7.9 %all_gather.7 = bf16[512,640]{1,0:T(8,128)(2,1)S(1)} all-gather(bf16[128,640]{1,0:T(8,128)(2,1)S(1)} %multiply_convert_fusion), channel_id=1, replica_groups=mesh['tok'=4,'vocab'=8] {'tok'}, dimensions={0}, use_global_device_ids=true | all-gather | bytes 819200 | tf_op jit(solution)/shard_map/all_gather | solution.py:34
  89.5 55.5 %reduce-scatter.4.cloned.1.call-done = f32[448,128]{1,0:T(8,128)} async-done(((f32[3584,128]{1,0:T(8,128)}), f32[448,128]{1,0:T(8,128)}) %reduce-scatter.4.cloned.1.call-update) | async-done | bytes 229392
  145.0 1.0 copy.13
  146.1 0.8 copy.10
  146.8 0.0 all-gather.2.cloned.1.call-done
  146.8 1.3 constant_dynamic-slice_fusion
  148.1 2.4 %convert_reduce_fusion = bf16[896,640]{1,0:T(8,128)(2,1)} fusion(bf16[4,128,896]{2,1,0:T(8,128)(2,1)S(1)} %bitcast.13, bf16[4,128,640]{2,1,0:T(8,128)(2,1)S(1)} %bitcast.14), kind=kOutput, calls=%fused_computation.1 | convolution fusion | flops 591216640 | bytes 2719744 | tf_op jit(solution)/shard_map/kti,ktv->kiv/dot_general | solution.py:39
Async XLA Ops:
  8.0 44.8 %copy-start = (bf16[128,3584]{1,0:T(8,128)(2,1)S(1)}, bf16[128,3584]{1,0:T(8,128)(2,1)}, u32[]{:S(2)}) copy-start(bf16[128,3584]{1,0:T(8,128)(2,1)} %param.5) | copy-start | bytes 2752516
  8.0 137.0 %reduce-scatter.4.cloned.1.call-start = ((), (), s32[]{:S(2)}) async-start(), calls=%async_computation.2 | async-start | bytes 2064384
  81.0 65.9 %all-gather.2.cloned.1.call-start = ((), (), s32[]{:S(2)}) async-start(), calls=%async_computation.1 | async-start | bytes 4587520 | tf_op jit(solution)/shard_map/all_gather | solution.py:33
Sparse Core Ops, SparseCore 0:
  81.1 63.8 reduce-scatter.3
Sparse Core Ops, SparseCore 1:
  83.0 28.6 all-gather.1
where the time goes:
time: 158 us
  blocking collectives  67.4 us (43%)
  waiting for transfers between devices  56.1 us (36%)
  between operations  15.5 us (10%)
  matrix products  13.1 us (8%)
  local copies, waits for them, and re-layouts  4.77 us (3%)
    unnamed x3, waiting for transfers between devices  56.1 us
    pmax x1, blocking collectives, local(): peak = lax.pmax(jnp.max(logits, axis=1), 'vocab')  23.2 us
    psum x1, blocking collectives, local(): mean = lax.psum(jnp.sum(probs * tangent, axis=1), 'vocab')  19.1 us
    psum x1, blocking collectives, local(): total = lax.psum(jnp.sum(expo, axis=1), 'vocab')  17.1 us
    all_gather x1, blocking collectives, local(): lax.all_gather(grads, 'tok', axis=0, tiled=True)  7.94 us
    dot_general x1, matrix products, local(): lax.dot_general(head_weight, grads, (((1,), (1,)), ((), ())), preferred_e...  3.85 us
    dot_general x1, matrix products, local(): jnp.dot(hidden_states, head_weight, preferred_element_type=jnp.float32)  3.55 us
    unnamed x5, local copies, waits for them, and re-layouts  3.52 us
  transfers between devices with their start and end apart: 2, of which 1 were waited for; matrix products, arithmetic and copies ran while one was open for 1% of the time, Pallas kernels for 0%

commit v1 on v0

--- a/solution.py
+++ b/solution.py
@@ -1,10 +1,276 @@
+import functools
+
 import jax
 import jax.numpy as jnp
 from jax import lax
+from jax.experimental import pallas as pl
+from jax.experimental.pallas import tpu as pltpu
 from jax.sharding import PartitionSpec as P
 
 TOK_DEV = 128
 BUCKETS = 8
+MESH = pl.DeviceIdType.MESH
+
+N_TOK = 4
+N_Z = 4
+N_Y = 2
+SUB = 2
+W_CHUNKS = 7
+ORDER = ((3, 2, 1, 0), (3, 2, 0, 1), (0, 1, 3, 2), (0, 1, 2, 3))
+
+
+def scale_of(buckets):
+    return 0.25 * jnp.exp2(buckets.astype(jnp.float32) * (3.0 / (BUCKETS - 1)))
+
+
+def by_z(z, values):
+    out = values[0]
+    for i in range(1, len(values)):
+        out = jnp.where(z == i, values[i], out)
+    return out
+
+
+def kernel(
+    h_ref, t_ref, b_ref, w_ref, cot_ref, wg_ref,
+    hh, w, acc, hall, gall, stats, own, ysend, yrecv, zsend, zrecv, wacc, wout,
+    load_sem, wload_sem, hs_sem, hr_sem, gs_sem, gr_sem, ss_sem, sr_sem,
+    ys_sem, yr_sem, zs_sem, zr_sem, out_sem,
+):
+    tok, voc = lax.axis_index("tok"), lax.axis_index("vocab")
+    x, core = tok // 2, tok % 2
+    z, y = voc // N_Y, voc % N_Y
+    tokens, width = h_ref.shape
+    vocab = w_ref.shape[1]
+    rows = hall.shape[2]
+    shard = cot_ref.shape[0]
+    piece = shard // SUB
+
+    def tok_peer(d):
+        return ((x + d // 2) % 2) * 2 + (core + d % 2) % 2
+
+    def voc_peer(d):
+        return (voc + d) % (N_Z * N_Y)
+
+    barrier = pltpu.get_barrier_semaphore()
+    for d in range(1, N_TOK):
+        pl.semaphore_signal(barrier, inc=1, device_id=(tok_peer(d), voc), device_id_type=MESH)
+    for d in range(1, N_Z * N_Y):
+        pl.semaphore_signal(barrier, inc=1, device_id=(tok, voc_peer(d)), device_id_type=MESH)
+
+    h_load = pltpu.make_async_copy(h_ref, hh.at[pl.ds(0, tokens)], load_sem.at[0])
+    t_load = pltpu.make_async_copy(t_ref, hh.at[pl.ds(tokens, tokens)], load_sem.at[1])
+    h_load.start()
+    t_load.start()
+    depth = width // W_CHUNKS
+    w_loads = []
+    for i in range(W_CHUNKS):
+        part = pl.ds(i * depth, depth)
+        load = pltpu.make_async_copy(w_ref.at[part], w.at[part], wload_sem.at[i])
+        load.start()
+        w_loads.append(load)
+
+    def columns_of(device):
+        return pl.ds(pl.multiple_of(device * rows, 128), rows)
+
+    mine = pltpu.make_async_copy(h_ref.at[:, columns_of(tok)], hall.at[0], load_sem.at[2])
+    mine.start()
+
+    pl.semaphore_wait(barrier, N_TOK - 1 + N_Z * N_Y - 1)
+
+    h_sends = []
+    for d in (1, 2, 3):
+        send = pltpu.make_async_remote_copy(
+            src_ref=h_ref.at[:, columns_of(tok_peer(d))], dst_ref=hall.at[d],
+            send_sem=hs_sem.at[d], recv_sem=hr_sem.at[d],
+            device_id=(tok_peer(d), voc), device_id_type=MESH,
+        )
+        send.start()
+        h_sends.append(send)
+
+    h_load.wait()
+    t_load.wait()
+    for i in range(W_CHUNKS):
+        w_loads[i].wait()
+        part = pl.ds(i * depth, depth)
+        term = jnp.dot(hh[:, part], w[part, :], preferred_element_type=jnp.float32)
+        if i == 0:
+            acc[...] = term
+        else:
+            acc[...] += term
+
+    logits, tangent = acc[pl.ds(0, tokens), :], acc[pl.ds(tokens, tokens), :]
+    peak = jnp.max(logits, axis=1, keepdims=True)
+    expo = jnp.exp(logits - peak)
+    total = jnp.sum(expo, axis=1, keepdims=True)
+    weighted = jnp.sum(expo * tangent, axis=1, keepdims=True)
+    acc[pl.ds(0, tokens), :] = expo
+    lane = lax.broadcasted_iota(jnp.int32, (tokens, 128), 1)
+    table = jnp.where(lane == 0, peak, jnp.where(lane == 1, total, weighted))
+    stats[0] = table.T[0:8, :]
+    stat_sends = []
+    for d in range(1, N_Z * N_Y):
+        send = pltpu.make_async_remote_copy(
+            src_ref=stats.at[0], dst_ref=stats.at[d],
+            send_sem=ss_sem.at[d], recv_sem=sr_sem.at[d],
+            device_id=(tok, voc_peer(d)), device_id_type=MESH,
+        )
+        send.start()
+        stat_sends.append(send)
+    scale = scale_of(b_ref[...])
+    for send in stat_sends:
+        send.wait()
+
+    all_stats = stats[...]
+    peaks, totals, sums = all_stats[:, 0, :], all_stats[:, 1, :], all_stats[:, 2, :]
+    top = jnp.max(peaks, axis=0, keepdims=True)
+    shrink = jnp.exp(peaks - top)
+    denominator = jnp.sum(totals * shrink, axis=0, keepdims=True)
+    mean = jnp.sum(sums * shrink, axis=0, keepdims=True) / denominator
+    factor = scale * shrink[0:1, :] / denominator
+    line = lax.broadcasted_iota(jnp.int32, (128, tokens), 0)
+    back = jnp.where(line == 0, factor, mean).T
+    grads = acc[pl.ds(0, tokens), :] * back[:, 0:1] * (acc[pl.ds(tokens, tokens), :] - back[:, 1:2])
+    gall[0] = grads.astype(jnp.bfloat16)
+    turned = grads.T.astype(jnp.bfloat16)
+
+    g_sends = []
+    for d in (1, 2, 3):
+        send = pltpu.make_async_remote_copy(
+            src_ref=gall.at[0], dst_ref=gall.at[d],
+            send_sem=gs_sem.at[d], recv_sem=gr_sem.at[d],
+            device_id=(tok_peer(d), voc), device_id_type=MESH,
+        )
+        send.start()
+        g_sends.append(send)
+
+    y_peer = z * N_Y + (1 - y)
+    orders = [by_z(z, [o[k] for o in ORDER]) for k in range(N_Z)]
+
+    def cotangent_of(k, side):
+        start = pl.multiple_of((orders[k] * N_Y + side) * shard, 16)
+        return jnp.dot(w[pl.ds(start, shard), :], turned, preferred_element_type=jnp.float32)
+
+    y_sends = []
+    for k in range(N_Z):
+        ysend[k] = cotangent_of(k, 1 - y).astype(jnp.bfloat16)
+        for s in range(SUB):
+            part = pl.ds(s * piece, piece)
+            send = pltpu.make_async_remote_copy(
+                src_ref=ysend.at[k, part], dst_ref=yrecv.at[k, part],
+                send_sem=ys_sem.at[k, s], recv_sem=yr_sem.at[k, s],
+                device_id=(tok, y_peer), device_id_type=MESH,
+            )
+            send.start()
+            y_sends.append(send)
+    for k in range(N_Z):
+        own[k] = cotangent_of(k, y)
+
+    def weight_term(pair):
+        h = hall[pl.ds(2 * pair, 2)].reshape(2 * tokens, rows)
+        g = gall[pl.ds(2 * pair, 2)].reshape(2 * tokens, vocab)
+        return lax.dot_general(h, g, (((0,), (0,)), ((), ())), preferred_element_type=jnp.float32)
+
+    def z_copy(zz, j, s, right):
+        part = pl.ds(s * piece, piece)
+        to = zz + 1 if right else zz - 1
+        return pltpu.make_async_remote_copy(
+            src_ref=zsend.at[j, part], dst_ref=zrecv.at[0 if right else 1, j, part],
+            send_sem=zs_sem.at[j, s], recv_sem=zr_sem.at[0 if right else 1, j, s],
+            device_id=(tok, min(max(to, 0), N_Z - 1) * N_Y + y), device_id_type=MESH,
+        )
+
+    def z_step(zz, k, s):
+        j = ORDER[zz][k]
+        part = pl.ds(s * piece, piece)
+        y_sends[k * SUB + s].wait_recv()
+        value = own[k, part] + yrecv[k, part].astype(jnp.float32)
+        if j >= zz and zz > 0:
+            z_copy(zz, j, s, True).wait_recv()
+            value = value + zrecv[0, j, part].astype(jnp.float32)
+        if j <= zz and zz < N_Z - 1:
+            z_copy(zz, j, s, False).wait_recv()
+            value = value + zrecv[1, j, part].astype(jnp.float32)
+        if j == zz:
+            cot_ref[part, :] = value.astype(jnp.bfloat16)
+        else:
+            zsend[j, part] = value.astype(jnp.bfloat16)
+            z_copy(zz, j, s, j > zz).start()
+
+    def z_steps(ks):
+        for zz in range(N_Z):
+            @pl.when(z == zz)
+            def _(zz=zz):
+                for k in ks:
+                    for s in range(SUB):
+                        z_step(zz, k, s)
+
+    mine.wait()
+    h_sends[0].wait()
+    g_sends[0].wait()
+    wacc[...] = weight_term(0)
+    z_steps((0, 1, 2))
+    for i in (1, 2):
+        h_sends[i].wait()
+        g_sends[i].wait()
+    wout[...] = (wacc[...] + weight_term(1)).astype(jnp.bfloat16)
+    out = pltpu.make_async_copy(wout, wg_ref, out_sem)
+    out.start()
+    z_steps((3,))
+
+    for send in y_sends:
+        send.wait_send()
+    for zz in range(N_Z):
+        @pl.when(z == zz)
+        def _(zz=zz):
+            for j in range(N_Z):
+                if j != zz:
+                    for s in range(SUB):
+                        z_copy(zz, j, s, j > zz).wait_send()
+    out.wait()
+
+
+def fused(hidden_states, hidden_tangent, buckets, head_weight):
+    tokens, width = hidden_states.shape
+    vocab = head_weight.shape[1]
+    rows, shard = width // N_TOK, width // (N_Z * N_Y)
+    bf16, f32 = jnp.bfloat16, jnp.float32
+    dma = pltpu.SemaphoreType.DMA
+    vmem = pl.BlockSpec(memory_space=pltpu.VMEM)
+    hbm = pl.BlockSpec(memory_space=pl.ANY)
+    return pl.pallas_call(
+        kernel,
+        out_shape=(
+            jax.ShapeDtypeStruct((shard, tokens), bf16),
+            jax.ShapeDtypeStruct((rows, vocab), bf16),
+        ),
+        in_specs=[hbm, hbm, vmem, hbm],
+        out_specs=(vmem, hbm),
+        scratch_shapes=[
+            pltpu.VMEM((2 * tokens, width), bf16),
+            pltpu.VMEM((width, vocab), bf16),
+            pltpu.VMEM((2 * tokens, vocab), f32),
+            pltpu.VMEM((N_TOK, tokens, rows), bf16),
+            pltpu.VMEM((N_TOK, tokens, vocab), bf16),
+            pltpu.VMEM((N_Z * N_Y, 8, tokens), f32),
+            pltpu.VMEM((N_Z, shard, tokens), f32),
+            pltpu.VMEM((N_Z, shard, tokens), bf16),
+            pltpu.VMEM((N_Z, shard, tokens), bf16),
+            pltpu.VMEM((N_Z, shard, tokens), bf16),
+            pltpu.VMEM((2, N_Z, shard, tokens), bf16),
+            pltpu.VMEM((rows, vocab), f32),
+            pltpu.VMEM((rows, vocab), bf16),
+            dma((3,)),
+            dma((W_CHUNKS,)),
+            dma((N_TOK,)), dma((N_TOK,)), dma((N_TOK,)), dma((N_TOK,)),
+            dma((N_Z * N_Y,)), dma((N_Z * N_Y,)),
+            dma((N_Z, SUB)), dma((N_Z, SUB)),
+            dma((N_Z, SUB)), dma((2, N_Z, SUB)),
+            dma,
+        ],
+        compiler_params=pltpu.CompilerParams(
+            collective_id=0, has_side_effects=True, vmem_limit_bytes=48 * 2**20
+        ),
+    )(hidden_states, hidden_tangent, buckets.reshape(1, tokens), head_weight)
 
 
 def local(hidden_states, hidden_tangent, buckets, head_weight):
@@ -15,7 +281,7 @@
     total = lax.psum(jnp.sum(expo, axis=1), "vocab")
     probs = expo / total[:, None]
     mean = lax.psum(jnp.sum(probs * tangent, axis=1), "vocab")
-    scale = 0.25 * jnp.exp2(buckets.astype(jnp.float32) * (3.0 / (BUCKETS - 1)))
+    scale = scale_of(buckets)
     grads = (scale[:, None] * probs * (tangent - mean[:, None])).astype(jnp.bfloat16)
     width = head_weight.shape[0]
     cotan = lax.psum_scatter(
@@ -44,8 +310,9 @@
 
 
 def solution(mesh):
+    small = mesh.shape["tok"] == N_TOK and mesh.shape["vocab"] == N_Z * N_Y
     return jax.shard_map(
-        local,
+        fused if small else local,
         mesh=mesh,
         in_specs=(P("tok", None), P("tok", None), P("tok"), P(None, "vocab")),
         out_specs=(P("vocab", "tok"), P("tok", "vocab")),

time: 158 us -> 34.8 us (0.22)
  blocking collectives: 67.4 us -> 0 us
  waiting for transfers between devices: 56.1 us -> 0 us
  Pallas kernels: 0 us -> 29.3 us
  between operations: 15.5 us -> 0.65 us
  matrix products: 13.1 us -> 0 us
    unnamed x3 -> x0, waiting for transfers between devices: 56.1 us -> none
    psum x2 -> x0, blocking collectives: 36.3 us -> none  [the longest x1 19.1 us: local(): mean = lax.psum(jnp.sum(probs * tangent, axis=1), 'vocab')]
    pallas_call x0 -> x1, Pallas kernels: none -> 29.3 us  [fused(): pl.pallas_call(kernel, out_shape=(jax.ShapeDtypeStruct((shard, tokens), b...]
    pmax x1 -> x0, blocking collectives: 23.2 us -> none  [local(): peak = lax.pmax(jnp.max(logits, axis=1), 'vocab')]
    dot_general x4 -> x0, matrix products: 13.1 us -> none  [the longest x1 3.85 us: local(): lax.dot_general(head_weight, grads, (((1,), (1,)), ((), ())), preferred_e...]
    all_gather x1 -> x0, blocking collectives: 7.94 us -> none  [local(): lax.all_gather(grads, 'tok', axis=0, tiled=True)]
    unnamed x5 -> x8, local copies, waits for them, and re-layouts: 3.52 us -> 4.66 us
  transfers between devices with their start and end apart: 2 -> 0, of which waited for: 1 -> 0; matrix products, arithmetic and copies ran while one was open for 1% -> 0% of each run, Pallas kernels for 0% -> 0%
where the time goes in v1:
time: 34.8 us; the launch traced here: 34.6 us
  Pallas kernels  29.3 us (84%)
  local copies, waits for them, and re-layouts  4.66 us (13%)
  between operations  0.65 us (2%)
    pallas_call x1, Pallas kernels, fused(): pl.pallas_call(kernel, out_shape=(jax.ShapeDtypeStruct((shard, tokens), b...  29.3 us
    unnamed x8, local copies, waits for them, and re-layouts  4.66 us

profile of v1, /device:TPU:0, one launch (start us, length us, event | category | flops | bytes accessed | tf_op | source)
XLA Modules:
  0.0 34.6 jit_solution(18179594103254190365)
XLA Ops:
  0.6 0.0 copy-start
  0.6 1.2 %copy-done = bf16[128,3584]{1,0:T(8,128)(2,1)S(1)} copy-done((bf16[128,3584]{1,0:T(8,128)(2,1)S(1)}, bf16[128,3584]{1,0:T(8,128)(2,1)}, u32[]{:S(2)}) %copy-start) | copy-done | bytes 917528
  1.8 0.0 copy-start.1
  1.8 1.2 %copy-done.1 = bf16[128,3584]{1,0:T(8,128)(2,1)S(1)} copy-done((bf16[128,3584]{1,0:T(8,128)(2,1)S(1)}, bf16[128,3584]{1,0:T(8,128)(2,1)}, u32[]{:S(2)}) %copy-start.1) | copy-done | bytes 917528
  3.0 0.0 copy-start.2
  3.0 0.7 %copy-done.2 = s32[128]{0:T(128)S(1)} copy-done((s32[128]{0:T(128)S(1)}, s32[128]{0:T(128)}, u32[]{:S(2)}) %copy-start.2) | copy-done | bytes 536
  3.6 29.3 %shard_map.59 = (bf16[448,128]{1,0:T(8,128)(2,1)S(1)}, bf16[896,640]{1,0:T(8,128)(2,1)S(1)}) custom-call(bf16[128,3584]{1,0:T(8,128)(2,1)S(1)} %copy-done, bf16[128,3584]{1,0:T(8,128)(2,1)S(1)} %copy-done.1, s32[1,128]{1,0:T(1,128)S(1)} %bitcast.1, bf16[3584,640]{1,0:T(8,128)(2,1)} %w_ref.1), custom_call_target="tpu_custom_call" | custom-call | tf_op jit(solution)/shard_map/pallas_call | solution.py:240
  33.0 0.6 %copy.8 = bf16[448,128]{1,0:T(8,128)(2,1)} copy(bf16[448,128]{1,0:T(8,128)(2,1)S(1)} %get-tuple-element.4) | data formatting | bytes 229376
  33.6 1.0 %copy.9 = bf16[896,640]{1,0:T(8,128)(2,1)} copy(bf16[896,640]{1,0:T(8,128)(2,1)S(1)} %get-tuple-element.5) | data formatting | bytes 2293760
Async XLA Ops:
  0.6 1.2 %copy-start = (bf16[128,3584]{1,0:T(8,128)(2,1)S(1)}, bf16[128,3584]{1,0:T(8,128)(2,1)}, u32[]{:S(2)}) copy-start(bf16[128,3584]{1,0:T(8,128)(2,1)} %h_ref.1) | copy-start | bytes 2752516
  1.8 1.2 %copy-start.1 = (bf16[128,3584]{1,0:T(8,128)(2,1)S(1)}, bf16[128,3584]{1,0:T(8,128)(2,1)}, u32[]{:S(2)}) copy-start(bf16[128,3584]{1,0:T(8,128)(2,1)} %t_ref.1) | copy-start | bytes 2752516
  3.0 0.7 %copy-start.2 = (s32[128]{0:T(128)S(1)}, s32[128]{0:T(128)}, u32[]{:S(2)}) copy-start(s32[128]{0:T(128)} %param.6) | copy-start | bytes 1540

commit v2 on v1

--- a/solution.py
+++ b/solution.py
@@ -31,8 +31,8 @@
 
 
 def kernel(
-    h_ref, t_ref, b_ref, w_ref, cot_ref, wg_ref,
-    hh, w, acc, hall, gall, stats, own, ysend, yrecv, zsend, zrecv, wacc, wout,
+    h_ref, t_ref, b_ref, w_ref, cot_out, wg_out,
+    bvec, cot, hh, w, acc, hall, gall, stats, own, ysend, yrecv, zsend, zrecv, wacc, wout,
     load_sem, wload_sem, hs_sem, hr_sem, gs_sem, gr_sem, ss_sem, sr_sem,
     ys_sem, yr_sem, zs_sem, zr_sem, out_sem,
 ):
@@ -42,7 +42,7 @@
     tokens, width = h_ref.shape
     vocab = w_ref.shape[1]
     rows = hall.shape[2]
-    shard = cot_ref.shape[0]
+    shard = cot.shape[0]
     piece = shard // SUB
 
     def tok_peer(d):
@@ -74,6 +74,8 @@
 
     mine = pltpu.make_async_copy(h_ref.at[:, columns_of(tok)], hall.at[0], load_sem.at[2])
     mine.start()
+    b_load = pltpu.make_async_copy(b_ref, bvec, load_sem.at[3])
+    b_load.start()
 
     pl.semaphore_wait(barrier, N_TOK - 1 + N_Z * N_Y - 1)
 
@@ -116,7 +118,8 @@
         )
         send.start()
         stat_sends.append(send)
-    scale = scale_of(b_ref[...])
+    b_load.wait()
+    scale = scale_of(bvec[...])
     for send in stat_sends:
         send.wait()
 
@@ -191,7 +194,7 @@
             z_copy(zz, j, s, False).wait_recv()
             value = value + zrecv[1, j, part].astype(jnp.float32)
         if j == zz:
-            cot_ref[part, :] = value.astype(jnp.bfloat16)
+            cot[part, :] = value.astype(jnp.bfloat16)
         else:
             zsend[j, part] = value.astype(jnp.bfloat16)
             z_copy(zz, j, s, j > zz).start()
@@ -213,9 +216,11 @@
         h_sends[i].wait()
         g_sends[i].wait()
     wout[...] = (wacc[...] + weight_term(1)).astype(jnp.bfloat16)
-    out = pltpu.make_async_copy(wout, wg_ref, out_sem)
+    out = pltpu.make_async_copy(wout, wg_out, out_sem.at[0])
     out.start()
     z_steps((3,))
+    cot_store = pltpu.make_async_copy(cot, cot_out, out_sem.at[1])
+    cot_store.start()
 
     for send in y_sends:
         send.wait_send()
@@ -227,6 +232,7 @@
                     for s in range(SUB):
                         z_copy(zz, j, s, j > zz).wait_send()
     out.wait()
+    cot_store.wait()
 
 
 def fused(hidden_states, hidden_tangent, buckets, head_weight):
@@ -235,17 +241,18 @@
     rows, shard = width // N_TOK, width // (N_Z * N_Y)
     bf16, f32 = jnp.bfloat16, jnp.float32
     dma = pltpu.SemaphoreType.DMA
-    vmem = pl.BlockSpec(memory_space=pltpu.VMEM)
-    hbm = pl.BlockSpec(memory_space=pl.ANY)
+    hbm = pl.BlockSpec(memory_space=pltpu.HBM)
     return pl.pallas_call(
         kernel,
         out_shape=(
             jax.ShapeDtypeStruct((shard, tokens), bf16),
             jax.ShapeDtypeStruct((rows, vocab), bf16),
         ),
-        in_specs=[hbm, hbm, vmem, hbm],
-        out_specs=(vmem, hbm),
+        in_specs=[hbm, hbm, hbm, hbm],
+        out_specs=(hbm, hbm),
         scratch_shapes=[
+            pltpu.VMEM((1, tokens), jnp.int32),
+            pltpu.VMEM((shard, tokens), bf16),
             pltpu.VMEM((2 * tokens, width), bf16),
             pltpu.VMEM((width, vocab), bf16),
             pltpu.VMEM((2 * tokens, vocab), f32),
@@ -259,16 +266,16 @@
             pltpu.VMEM((2, N_Z, shard, tokens), bf16),
             pltpu.VMEM((rows, vocab), f32),
             pltpu.VMEM((rows, vocab), bf16),
-            dma((3,)),
+            dma((4,)),
             dma((W_CHUNKS,)),
             dma((N_TOK,)), dma((N_TOK,)), dma((N_TOK,)), dma((N_TOK,)),
             dma((N_Z * N_Y,)), dma((N_Z * N_Y,)),
             dma((N_Z, SUB)), dma((N_Z, SUB)),
             dma((N_Z, SUB)), dma((2, N_Z, SUB)),
-            dma,
+            dma((2,)),
         ],
         compiler_params=pltpu.CompilerParams(
-            collective_id=0, has_side_effects=True, vmem_limit_bytes=48 * 2**20
+            collective_id=0, has_side_effects=True, vmem_limit_bytes=60 * 2**20
         ),
     )(hidden_states, hidden_tangent, buckets.reshape(1, tokens), head_weight)
 

time: 34.8 us -> 34.7 us (level)
  local copies, waits for them, and re-layouts: 4.66 us -> 3.91 us
  Pallas kernels: 29.3 us -> 30 us
    unnamed x8 -> x2, local copies, waits for them, and re-layouts: 4.66 us -> 3.91 us
    pallas_call x1, Pallas kernels: 29.3 us -> 30 us  [fused(): pl.pallas_call(kernel, out_shape=(jax.ShapeDtypeStruct((shard, tokens), b...]
where the time goes in v2:
time: 34.7 us; the launch traced here: 34.5 us
  Pallas kernels  30 us (86%)
  local copies, waits for them, and re-layouts  3.91 us (11%)
  between operations  0.64 us (2%)
    pallas_call x1, Pallas kernels, fused(): pl.pallas_call(kernel, out_shape=(jax.ShapeDtypeStruct((shard, tokens), b...  30 us
    unnamed x2, local copies, waits for them, and re-layouts  3.91 us

profile of v2, /device:TPU:0, one launch (start us, length us, event | category | flops | bytes accessed | tf_op | source)
XLA Modules:
  0.0 34.5 jit_solution(11060287987084975321)
XLA Ops:
  0.6 30.0 %shard_map.59 = (bf16[448,128]{1,0:T(8,128)(2,1)}, bf16[896,640]{1,0:T(8,128)(2,1)}) custom-call(bf16[128,3584]{1,0:T(8,128)(2,1)} %h_ref.1, bf16[128,3584]{1,0:T(8,128)(2,1)} %t_ref.1, s32[1,128]{1,0:T(1,128)} %bitcast.1, bf16[3584,640]{1,0:T(8,128)(2,1)} %w_ref.1), custom_call_target="tpu_custom_call" | custom-call | tf_op jit(solution)/shard_map/pallas_call | solution.py:245
  30.6 1.6 %copy.8 = bf16[448,128]{1,0:T(8,128)(2,1)} copy(bf16[448,128]{1,0:T(8,128)(2,1)} %get-tuple-element.4) | data formatting | bytes 229376
  32.2 2.4 %copy.9 = bf16[896,640]{1,0:T(8,128)(2,1)} copy(bf16[896,640]{1,0:T(8,128)(2,1)} %get-tuple-element.5) | data formatting | bytes 2293760

commit v3 on v2

--- a/solution.py
+++ b/solution.py
@@ -15,7 +15,8 @@
 N_Z = 4
 N_Y = 2
 SUB = 2
-W_CHUNKS = 7
+W_CHUNKS = 4
+PARTS = 7
 ORDER = ((3, 2, 1, 0), (3, 2, 0, 1), (0, 1, 3, 2), (0, 1, 2, 3))
 
 
@@ -77,21 +78,21 @@
     b_load = pltpu.make_async_copy(b_ref, bvec, load_sem.at[3])
     b_load.start()
 
-    pl.semaphore_wait(barrier, N_TOK - 1 + N_Z * N_Y - 1)
-
-    h_sends = []
-    for d in (1, 2, 3):
-        send = pltpu.make_async_remote_copy(
-            src_ref=h_ref.at[:, columns_of(tok_peer(d))], dst_ref=hall.at[d],
-            send_sem=hs_sem.at[d], recv_sem=hr_sem.at[d],
-            device_id=(tok_peer(d), voc), device_id_type=MESH,
-        )
-        send.start()
-        h_sends.append(send)
-
     h_load.wait()
     t_load.wait()
     for i in range(W_CHUNKS):
+        if i == W_CHUNKS // 2:
+            pl.semaphore_wait(barrier, N_TOK - 1 + N_Z * N_Y - 1)
+
+            h_sends = []
+            for d in (1, 2, 3):
+                send = pltpu.make_async_remote_copy(
+                    src_ref=h_ref.at[:, columns_of(tok_peer(d))], dst_ref=hall.at[d],
+                    send_sem=hs_sem.at[d], recv_sem=hr_sem.at[d],
+                    device_id=(tok_peer(d), voc), device_id_type=MESH,
+                )
+                send.start()
+                h_sends.append(send)
         w_loads[i].wait()
         part = pl.ds(i * depth, depth)
         term = jnp.dot(hh[:, part], w[part, :], preferred_element_type=jnp.float32)
@@ -235,6 +236,23 @@
     cot_store.wait()
 
 
+def store(cot, wg, cot_out, wg_out, cot_held, wg_held, in_sem, out_sem):
+    part = wg.shape[0] // PARTS
+    moves = [(cot, cot_held, cot_out)]
+    for i in range(PARTS):
+        at = pl.ds(i * part, part)
+        moves.append((wg.at[at], wg_held.at[at], wg_out.at[at]))
+    loads = [pltpu.make_async_copy(a, b, in_sem.at[i]) for i, (a, b, _) in enumerate(moves)]
+    saves = [pltpu.make_async_copy(b, c, out_sem.at[i]) for i, (_, b, c) in enumerate(moves)]
+    for load in loads:
+        load.start()
+    for load, save in zip(loads, saves):
+        load.wait()
+        save.start()
+    for save in saves:
+        save.wait()
+
+
 def fused(hidden_states, hidden_tangent, buckets, head_weight):
     tokens, width = hidden_states.shape
     vocab = head_weight.shape[1]
@@ -242,7 +260,7 @@
     bf16, f32 = jnp.bfloat16, jnp.float32
     dma = pltpu.SemaphoreType.DMA
     hbm = pl.BlockSpec(memory_space=pltpu.HBM)
-    return pl.pallas_call(
+    results = pl.pallas_call(
         kernel,
         out_shape=(
             jax.ShapeDtypeStruct((shard, tokens), bf16),
@@ -278,6 +296,17 @@
             collective_id=0, has_side_effects=True, vmem_limit_bytes=60 * 2**20
         ),
     )(hidden_states, hidden_tangent, buckets.reshape(1, tokens), head_weight)
+    return pl.pallas_call(
+        store,
+        out_shape=tuple(jax.ShapeDtypeStruct(r.shape, bf16) for r in results),
+        in_specs=[hbm, hbm],
+        out_specs=(hbm, hbm),
+        scratch_shapes=[
+            pltpu.VMEM((shard, tokens), bf16), pltpu.VMEM((rows, vocab), bf16),
+            dma((PARTS + 1,)), dma((PARTS + 1,)),
+        ],
+        compiler_params=pltpu.CompilerParams(vmem_limit_bytes=60 * 2**20),
+    )(*results)
 
 
 def local(hidden_states, hidden_tangent, buckets, head_weight):

time: 34.7 us -> 31.5 us (0.908)
  local copies, waits for them, and re-layouts: 3.91 us -> 0 us
  Pallas kernels: 30 us -> 30.7 us
    unnamed x2 -> x0, local copies, waits for them, and re-layouts: 3.91 us -> none
    pallas_call x0 -> x1, Pallas kernels: none -> 2.18 us  [fused(): pl.pallas_call(store, out_shape=tuple((jax.ShapeDtypeStruct(r.shape, bf16...]
    pallas_call x1, Pallas kernels: 30 us -> 28.5 us  [fused(): pl.pallas_call(kernel, out_shape=(jax.ShapeDtypeStruct((shard, tokens), b...]
where the time goes in v3:
time: 31.5 us; the launch traced here: 31.3 us
  Pallas kernels  30.7 us (97%)
  between operations  0.64 us (2%)
    pallas_call x1, Pallas kernels, fused(): pl.pallas_call(kernel, out_shape=(jax.ShapeDtypeStruct((shard, tokens), b...  28.5 us
    pallas_call x1, Pallas kernels, fused(): pl.pallas_call(store, out_shape=tuple((jax.ShapeDtypeStruct(r.shape, bf16...  2.18 us

profile of v3, /device:TPU:0, one launch (start us, length us, event | category | flops | bytes accessed | tf_op | source)
XLA Modules:
  0.0 31.3 jit_solution(11211294073365516225)
XLA Ops:
  0.6 28.5 %shard_map.59 = (bf16[448,128]{1,0:T(8,128)(2,1)}, bf16[896,640]{1,0:T(8,128)(2,1)}) custom-call(bf16[128,3584]{1,0:T(8,128)(2,1)} %h_ref.1, bf16[128,3584]{1,0:T(8,128)(2,1)} %t_ref.1, s32[1,128]{1,0:T(1,128)} %bitcast.1, bf16[3584,640]{1,0:T(8,128)(2,1)} %w_ref.1), custom_call_target="tpu_custom_call" | custom-call | tf_op jit(solution)/shard_map/pallas_call | solution.py:263
  29.1 2.2 %shard_map.60 = (bf16[448,128]{1,0:T(8,128)(2,1)}, bf16[896,640]{1,0:T(8,128)(2,1)}) custom-call(bf16[448,128]{1,0:T(8,128)(2,1)} %get-tuple-element.4.cot, bf16[896,640]{1,0:T(8,128)(2,1)} %get-tuple-element.5.wg), custom_call_target="tpu_custom_call" | custom-call | tf_op jit(solution)/shard_map/pallas_call | solution.py:299

commit v4 on v3

--- a/solution.py
+++ b/solution.py
@@ -14,7 +14,7 @@
 N_TOK = 4
 N_Z = 4
 N_Y = 2
-SUB = 2
+SUB = 4
 W_CHUNKS = 4
 PARTS = 7
 ORDER = ((3, 2, 1, 0), (3, 2, 0, 1), (0, 1, 3, 2), (0, 1, 2, 3))

time: 31.5 us -> 31.2 us (level)
  no operation moved by 1% of the time
where the time goes in v4:
time: 31.2 us; the launch traced here: 31.1 us
  Pallas kernels  30.4 us (97%)
  between operations  0.64 us (2%)
    pallas_call x1, Pallas kernels, fused(): pl.pallas_call(kernel, out_shape=(jax.ShapeDtypeStruct((shard, tokens), b...  28.2 us
    pallas_call x1, Pallas kernels, fused(): pl.pallas_call(store, out_shape=tuple((jax.ShapeDtypeStruct(r.shape, bf16...  2.18 us

profile of v4, /device:TPU:0, one launch (start us, length us, event | category | flops | bytes accessed | tf_op | source)
XLA Modules:
  0.0 31.1 jit_solution(6846117323530845702)
XLA Ops:
  0.6 28.2 %shard_map.59 = (bf16[448,128]{1,0:T(8,128)(2,1)}, bf16[896,640]{1,0:T(8,128)(2,1)}) custom-call(bf16[128,3584]{1,0:T(8,128)(2,1)} %h_ref.1, bf16[128,3584]{1,0:T(8,128)(2,1)} %t_ref.1, s32[1,128]{1,0:T(1,128)} %bitcast.1, bf16[3584,640]{1,0:T(8,128)(2,1)} %w_ref.1), custom_call_target="tpu_custom_call" | custom-call | tf_op jit(solution)/shard_map/pallas_call | solution.py:263
  28.9 2.2 %shard_map.60 = (bf16[448,128]{1,0:T(8,128)(2,1)}, bf16[896,640]{1,0:T(8,128)(2,1)}) custom-call(bf16[448,128]{1,0:T(8,128)(2,1)} %get-tuple-element.4.cot, bf16[896,640]{1,0:T(8,128)(2,1)} %get-tuple-element.5.wg), custom_call_target="tpu_custom_call" | custom-call | tf_op jit(solution)/shard_map/pallas_call | solution.py:299
